TPU v7x, 256 devices: a whole 4x4x8 slice. The times are simulated.
256 devices in a mesh: gy: 64 (over x, y, z_hi, core), gz: 4 (over z_lo).
Axes of the slice: x: 4, y: 4, z: 8 (z_hi: 2, z_lo: 4; z = z_hi * 4 + z_lo), core: 2. Of those that a mesh axis runs over, the one named last changes fastest.
Arguments:
- efield_check: bfloat16 [3, 2048, 8, 1024], P(None, 'gy', None, 'gz'), may hold values from -6 to 6
- hfield_check: bfloat16 [3, 2048, 8, 1024], P(None, 'gy', None, 'gz'), may hold values from -6 to 6
- polar_check: bfloat16 [3, 2048, 8, 1024], P(None, 'gy', None, 'gz'), may hold values from -4 to 4
- rate_check: bfloat16 [3, 2048, 8, 1024], P(None, 'gy', None, 'gz'), may hold values from -4 to 4
- levels_check: bfloat16 [2, 2048, 8, 1024], P(None, 'gy', None, 'gz'), may hold values from 0.049804688 to 0.5
- efield_seed: float32 [3, 2048, 8, 1024], P(None, 'gy', None, 'gz'), may hold values from -6 to 6
- hfield_seed: float32 [3, 2048, 8, 1024], P(None, 'gy', None, 'gz'), may hold values from -6 to 6
- polar_seed: float32 [3, 2048, 8, 1024], P(None, 'gy', None, 'gz'), may hold values from -6 to 6
- rate_seed: float32 [3, 2048, 8, 1024], P(None, 'gy', None, 'gz'), may hold values from -6 to 6
- levels_seed: float32 [2, 2048, 8, 1024], P(None, 'gy', None, 'gz'), may hold values from -6 to 6
- material_labels: int32 [2048, 8, 1024], P('gy', None, 'gz'), may hold values from 0 to 3
- gain_labels: int32 [2048, 8, 1024], P('gy', None, 'gz'), may hold values 0 or 1
- inverse_table: float32 [4], replicated, may hold values from 0.08 to 1
- source_field: float32 [2048, 8, 1024], P('gy', None, 'gz'), may hold values from -6 to 6
- start_step: int32 [1], replicated, may hold values from 0 to 255
Outputs:
- efield_grad: float32 [3, 2048, 8, 1024], P(None, 'gy', None, 'gz')
- hfield_grad: float32 [3, 2048, 8, 1024], P(None, 'gy', None, 'gz')
- polar_grad: float32 [3, 2048, 8, 1024], P(None, 'gy', None, 'gz')
- rate_grad: float32 [3, 2048, 8, 1024], P(None, 'gy', None, 'gz')
- levels_grad: float32 [2, 2048, 8, 1024], P(None, 'gy', None, 'gz')
- cell_grad: float32 [2048, 8, 1024], P('gy', None, 'gz')
- table_grad: float32 [4], replicated
All inputs are finite; a program needn't handle non-finite values. No bound on the sum of `gain_labels` on one device may be relied on, other than what follows from the above.
Results may differ from a plain program's by a relative error of at most 0.0003.
Values may be sent and summed in bfloat16 or wider, within the bound.
No kernel may reach another device: no remote copies, remote signals or barrier semaphores. Data moves between devices by JAX's collectives and lax.ppermute only.
A program may use at most 64 MiB of HBM per device.

v0:
```python
import math
import jax
import jax.numpy as jnp
from jax import lax
from jax.sharding import PartitionSpec as P

MAGNETIC_STEP = 0.5
ELECTRIC_STEP = 0.5
TIME_STEP = 0.5
DAMPING = 0.9
STIFFNESS = 0.3
COUPLING = 0.4
PUMPING = 0.05
UPPER_DECAY = 0.02
LOWER_DECAY = 0.3
STIMULATED = 0.2
SOURCE_OMEGA = 0.35


def shifted(block, axis, distance):
    devices = range(lax.axis_size(axis))
    route = [(i - distance, i) for i in devices if i - distance in devices]
    return lax.ppermute(block, axis, route)


def front(values, axis):
    rest = lax.slice_in_dim(values, 1, values.shape[axis], axis=axis)
    border = jnp.zeros_like(lax.slice_in_dim(values, 0, 1, axis=axis))
    return jnp.concatenate([rest, border], axis)


def behind(values, axis):
    rest = lax.slice_in_dim(values, 0, values.shape[axis] - 1, axis=axis)
    border = jnp.zeros_like(lax.slice_in_dim(values, 0, 1, axis=axis))
    return jnp.concatenate([border, rest], axis)


def curl_from(along_x, along_y, along_z):
    return jnp.stack([along_y[2] - along_z[1], along_z[0] - along_x[2], along_x[1] - along_y[0]])


def curl_forward(field):
    front_row = shifted(field[:, :1], "gy", -1)
    front_column = shifted(field[:, :, :, :1], "gz", -1)
    along_y = jnp.concatenate([field[:, 1:], front_row], 1) - field
    along_z = jnp.concatenate([field[:, :, :, 1:], front_column], 3) - field
    along_x = front(field, 2) - field
    return curl_from(along_x, along_y, along_z)


def curl_backward(field):
    back_row = shifted(field[:, -1:], "gy", 1)
    back_column = shifted(field[:, :, :, -1:], "gz", 1)
    along_y = field - jnp.concatenate([back_row, field[:, :-1]], 1)
    along_z = field - jnp.concatenate([back_column, field[:, :, :, :-1]], 3)
    along_x = field - behind(field, 2)
    return curl_from(along_x, along_y, along_z)


def local_update(
    efield, polar_field, polar_rate, levels, curl_field, inverse, gain_region, source_push
):
    rate_next = (
        DAMPING * polar_rate
        - STIFFNESS * polar_field
        + COUPLING * gain_region * (levels[0] - levels[1]) * efield
    )
    polar_next = polar_field + TIME_STEP * rate_next
    forcing = ELECTRIC_STEP * curl_field - (polar_next - polar_field)
    forcing = jnp.concatenate([forcing[:2], forcing[2:] - source_push[None]], 0)
    efield_next = efield + inverse * forcing
    stimulated = STIMULATED * gain_region * jnp.sum(efield_next * rate_next, axis=0)
    upper = (
        levels[0]
        + TIME_STEP * (PUMPING * (1.0 - levels[0] - levels[1]) - UPPER_DECAY * levels[0])
        - stimulated
    )
    lower = levels[1] + TIME_STEP * (UPPER_DECAY * levels[0] - LOWER_DECAY * levels[1]) + stimulated
    return (efield_next, polar_next, rate_next, jnp.stack([upper, lower]))


def reverse_local(
    efield, polar_field, polar_rate, levels, curl_field, inverse, gain_region, source_push, seeds
):

    def update(first, second, third, fourth, fifth, sixth):
        return local_update(first, second, third, fourth, fifth, sixth, gain_region, source_push)

    unused, pullback = jax.vjp(update, efield, polar_field, polar_rate, levels, curl_field, inverse)
    return pullback(seeds)


def material_map(material_labels, inverse_table):
    inverse = jnp.zeros(material_labels.shape, jnp.float32)
    for label in range(inverse_table.shape[0]):
        inverse = inverse + jnp.where(
            material_labels == label, inverse_table[label], jnp.float32(0.0)
        )
    return inverse


def label_sums(material_labels, values, count):
    return jnp.stack(
        [
            jnp.sum(jnp.where(material_labels == label, values, jnp.float32(0.0)))
            for label in range(count)
        ]
    )


def step_total(material_labels, values, count):
    return lax.psum(label_sums(material_labels, values, count), ("gy", "gz"))


def on_device(
    efield_check,
    hfield_check,
    polar_check,
    rate_check,
    levels_check,
    efield_seed,
    hfield_seed,
    polar_seed,
    rate_seed,
    levels_seed,
    material_labels,
    gain_labels,
    inverse_table,
    source_field,
    start_step,
):
    count = inverse_table.shape[0]
    inverse = material_map(material_labels, inverse_table)
    gain_region = gain_labels.astype(jnp.float32)
    start = start_step[0].astype(jnp.float32)
    first_sine = jnp.sin(SOURCE_OMEGA * start)
    push_first = first_sine * source_field
    push_second = jnp.sin(SOURCE_OMEGA * (start + 1.0)) * source_field
    efield = efield_check.astype(jnp.float32)
    polar_field = polar_check.astype(jnp.float32)
    polar_rate = rate_check.astype(jnp.float32)
    levels = levels_check.astype(jnp.float32)
    hfield = hfield_check.astype(jnp.float32)
    hfield_mid = hfield - MAGNETIC_STEP * curl_forward(efield)
    curl_first = curl_backward(hfield_mid)
    state_one = local_update(
        efield, polar_field, polar_rate, levels, curl_first, inverse, gain_region, push_first
    )
    hfield_next = hfield_mid - MAGNETIC_STEP * curl_forward(state_one[0])
    curl_second = curl_backward(hfield_next)
    back_e, back_p, back_q, back_n, back_c, grad_second = reverse_local(
        state_one[0],
        state_one[1],
        state_one[2],
        state_one[3],
        curl_second,
        inverse,
        gain_region,
        push_second,
        (efield_seed, polar_seed, rate_seed, levels_seed),
    )
    h_back = hfield_seed + curl_forward(back_c)
    e_back = back_e - MAGNETIC_STEP * curl_backward(h_back)
    last_e, polar_grad, rate_grad, levels_grad, last_c, grad_first = reverse_local(
        efield,
        polar_field,
        polar_rate,
        levels,
        curl_first,
        inverse,
        gain_region,
        push_first,
        (e_back, back_p, back_q, back_n),
    )
    hfield_grad = h_back + curl_forward(last_c)
    efield_grad = last_e - MAGNETIC_STEP * curl_backward(hfield_grad)
    cell_grad = grad_second + grad_first
    cells = (
        material_labels.shape[0]
        * material_labels.shape[1]
        * material_labels.shape[2]
        * lax.axis_size("gy")
        * lax.axis_size("gz")
    )
    totals = step_total(material_labels, grad_second, count) + step_total(
        material_labels, grad_first, count
    )
    table_grad = totals * (1.0 / math.sqrt(cells))
    return (efield_grad, hfield_grad, polar_grad, rate_grad, levels_grad, cell_grad, table_grad)


def solution(mesh):
    placed = (
        P(None, "gy", None, "gz"),
        P(None, "gy", None, "gz"),
        P(None, "gy", None, "gz"),
        P(None, "gy", None, "gz"),
        P(None, "gy", None, "gz"),
        P(None, "gy", None, "gz"),
        P(None, "gy", None, "gz"),
        P(None, "gy", None, "gz"),
        P(None, "gy", None, "gz"),
        P(None, "gy", None, "gz"),
        P("gy", None, "gz"),
        P("gy", None, "gz"),
        P(),
        P("gy", None, "gz"),
        P(),
    )
    return jax.shard_map(
        on_device,
        mesh=mesh,
        in_specs=placed,
        out_specs=(
            P(None, "gy", None, "gz"),
            P(None, "gy", None, "gz"),
            P(None, "gy", None, "gz"),
            P(None, "gy", None, "gz"),
            P(None, "gy", None, "gz"),
            P("gy", None, "gz"),
            P(),
        ),
        check_vma=False,
    )
```

profile of v0, /device:TPU:2, one launch (start us, length us, event | category | flops | bytes accessed | tf_op | source)
XLA Modules:
  0.0 215.5 jit_solution(16821565105719444470)
XLA Ops:
  1.7 1.3 collective-permute-start.1
  3.0 11.0 %collective-permute-start = (f32[3,1,8,256]{3,2,1,0:T(8,128)S(1)}, f32[3,1,8,256]{3,2,1,0:T(8,128)S(1)}, u32[]{:S(2)}, u32[]{:S(2)}) collective-permute-start(f32[3,1,8,256]{3,2,1,0:T(8,128)S(1)} %slice.410), channel_id=1, source_target_pairs={{4,0},{8,4},{12,8},{16,12},{20,16},{24,20},{28,24},{32,28},{36,32}... | collective-permute-start | bytes 73736 | tf_op jit(solution)/shard_map/ppermute | solution.py:23
  17.4 4.3 %collective-permute-start.3 = (f32[3,32,8,1]{3,2,1,0:T(8,128)S(1)}, f32[3,32,8,1]{3,2,1,0:T(8,128)S(1)}, u32[]{:S(2)}, u32[]{:S(2)}) collective-permute-start(f32[3,32,8,1]{3,2,1,0:T(8,128)S(1)} %slice.423), channel_id=1, source_target_pairs={{0,1},{1,2},{2,3},{4,5},{5,6},{6,7},{8,9},{9,10},{10,11},{12,13},{... | collective-permute-start | bytes 9224 | tf_op jit(solution)/shard_map/ppermute | solution.py:23
  21.7 5.1 %collective-permute-start.2 = (f32[3,1,8,256]{3,2,1,0:T(8,128)S(1)}, f32[3,1,8,256]{3,2,1,0:T(8,128)S(1)}, u32[]{:S(2)}, u32[]{:S(2)}) collective-permute-start(f32[3,1,8,256]{3,2,1,0:T(8,128)S(1)} %slice.420), channel_id=1, source_target_pairs={{0,4},{4,8},{8,12},{12,16},{16,20},{20,24},{24,28},{28,32},{32,36}... | collective-permute-start | bytes 73736 | tf_op jit(solution)/shard_map/ppermute | solution.py:23
  26.8 2.8 %select_add_fusion.2 = (f32[32,8,256]{2,1,0:T(8,128)S(1)}, pred[32,8,256]{2,1,0:T(8,128)(4,1)S(1)}, pred[32,8,256]{2,1,0:T(8,128)(4,1)S(1)}, pred[32,8,256]{2,1,...) fusion(f32[]{:T(128)} %bitcast.6, f32[]{:T(128)} %bitcast.5, f32[]{:T(128)} %bitcast.4, ...), kind=kLoop, calls=%fused_computation.118 | loop fusion | flops 983040 | bytes 1835024 | tf_op jit(solution)/shard_map/add | solution.py:96
  30.5 8.8 %collective-permute-done.2 = f32[3,1,8,256]{3,2,1,0:T(8,128)S(1)} collective-permute-done((f32[3,1,8,256]{3,2,1,0:T(8,128)S(1)}, f32[3,1,8,256]{3,2,1,0:T(8,128)S(1)}, u32[]{:S(2)}, u32[]{:S(2)}) %collective-permute-start.2) | collective-permute-done | bytes 24608 | tf_op jit(solution)/shard_map/ppermute | solution.py:23
  42.5 1.4 collective-permute-start.5
  43.9 1.9 collective-permute-start.4
  46.5 5.8 %collective-permute-done.5 = f32[3,32,8,1]{3,2,1,0:T(8,128)S(1)} collective-permute-done((f32[3,32,8,1]{3,2,1,0:T(8,128)S(1)}, f32[3,32,8,1]{3,2,1,0:T(8,128)S(1)}, u32[]{:S(2)}, u32[]{:S(2)}) %collective-permute-start.5) | collective-permute-done | bytes 3104 | tf_op jit(solution)/shard_map/ppermute | solution.py:23
  53.0 2.0 collective-permute-start.7
  55.0 1.9 collective-permute-start.6
  57.2 5.5 %collective-permute-done.7 = f32[3,32,8,1]{3,2,1,0:T(8,128)S(1)} collective-permute-done((f32[3,32,8,1]{3,2,1,0:T(8,128)S(1)}, f32[3,32,8,1]{3,2,1,0:T(8,128)S(1)}, u32[]{:S(2)}, u32[]{:S(2)}) %collective-permute-start.7) | collective-permute-done | bytes 3104 | tf_op jit(solution)/shard_map/ppermute | solution.py:23
  62.8 7.7 %collective-permute-done.6 = f32[3,1,8,256]{3,2,1,0:T(8,128)S(1)} collective-permute-done((f32[3,1,8,256]{3,2,1,0:T(8,128)S(1)}, f32[3,1,8,256]{3,2,1,0:T(8,128)S(1)}, u32[]{:S(2)}, u32[]{:S(2)}) %collective-permute-start.6) | collective-permute-done | bytes 24608 | tf_op jit(solution)/shard_map/ppermute | solution.py:23
  75.1 1.3 collective-permute-start.9
  76.4 1.9 collective-permute-start.8
  79.8 5.0 %collective-permute-done.9 = f32[3,32,8,1]{3,2,1,0:T(8,128)S(1)} collective-permute-done((f32[3,32,8,1]{3,2,1,0:T(8,128)S(1)}, f32[3,32,8,1]{3,2,1,0:T(8,128)S(1)}, u32[]{:S(2)}, u32[]{:S(2)}) %collective-permute-start.9) | collective-permute-done | bytes 3104 | tf_op jit(solution)/shard_map/ppermute | solution.py:23
  85.3 1.1 copy-done.2
  86.7 2.0 collective-permute-start.11
  88.8 1.9 collective-permute-start.10
  90.8 4.8 %collective-permute-done.11 = f32[3,32,8,1]{3,2,1,0:T(8,128)S(1)} collective-permute-done((f32[3,32,8,1]{3,2,1,0:T(8,128)S(1)}, f32[3,32,8,1]{3,2,1,0:T(8,128)S(1)}, u32[]{:S(2)}, u32[]{:S(2)}) %collective-permute-start.11) | collective-permute-done | bytes 3104 | tf_op jit(solution)/shard_map/ppermute | solution.py:23
  95.6 7.6 %collective-permute-done.10 = f32[3,1,8,256]{3,2,1,0:T(8,128)S(1)} collective-permute-done((f32[3,1,8,256]{3,2,1,0:T(8,128)S(1)}, f32[3,1,8,256]{3,2,1,0:T(8,128)S(1)}, u32[]{:S(2)}, u32[]{:S(2)}) %collective-permute-start.10) | collective-permute-done | bytes 24608 | tf_op jit(solution)/shard_map/ppermute | solution.py:23
  104.9 1.6 multiply_add_fusion
  107.4 1.3 collective-permute-start.13
  108.7 2.1 collective-permute-start.12
  110.8 1.6 select_reduce_fusion.7
  112.4 5.1 %maximum_add_fusion.2 = f32[4]{0:T(128)S(1)} fusion(f32[1]{0:T(128)} %bitcast.19, f32[1]{0:T(128)} %bitcast.18, f32[1]{0:T(128)} %bitcast.17, f32[1]{0:T(128)} %bitcast.16, f32[1]{0:T(128)} %bitcast.23, f32[1]{0:T(128)} %bitcast.22, f32[1]{0:T(128)} %bitcast.21, f32[1]{0:T(128)} %bitcast.20), kind=kLoop, calls=%fused_computation.132 | loop fusion | flops 28 | bytes 48 | tf_op jit(solution)/shard_map/add | solution.py:185
  118.7 76.3 %psum.16 = f32[4]{0:T(128)S(1)} all-reduce(f32[4]{0:T(128)S(1)} %maximum_add_fusion.2), channel_id=1, replica_groups=mesh['gy'=64,'gz'=4] {'gy','gz'}, use_global_device_ids=true, to_apply=%region_9.10 | all-reduce | flops 4 | bytes 32 | tf_op jit(solution)/shard_map/psum | solution.py:112
  195.4 1.3 maximum_subtract_fusion.11
  198.1 2.1 collective-permute-start.15
  200.2 1.9 collective-permute-start.14
  202.7 6.1 %collective-permute-done.15 = f32[3,32,8,1]{3,2,1,0:T(8,128)S(1)} collective-permute-done((f32[3,32,8,1]{3,2,1,0:T(8,128)S(1)}, f32[3,32,8,1]{3,2,1,0:T(8,128)S(1)}, u32[]{:S(2)}, u32[]{:S(2)}) %collective-permute-start.15) | collective-permute-done | bytes 3104 | tf_op jit(solution)/shard_map/ppermute | solution.py:23
  208.8 5.1 %collective-permute-done.14 = f32[3,1,8,256]{3,2,1,0:T(8,128)S(1)} collective-permute-done((f32[3,1,8,256]{3,2,1,0:T(8,128)S(1)}, f32[3,1,8,256]{3,2,1,0:T(8,128)S(1)}, u32[]{:S(2)}, u32[]{:S(2)}) %collective-permute-start.14) | collective-permute-done | bytes 24608 | tf_op jit(solution)/shard_map/ppermute | solution.py:23
  (130 shorter events, 23.5 us)
Async XLA Ops:
  0.6 2.3 %copy-start = (bf16[3,32,8,256]{3,2,1,0:T(8,128)(2,1)S(1)}, bf16[3,32,8,256]{3,2,1,0:T(8,128)(2,1)}, u32[]{:S(2)}) copy-start(bf16[3,32,8,256]{3,2,1,0:T(8,128)(2,1)} %param.15) | copy-start | bytes 1179652
  1.7 14.2 %collective-permute-start.1 = (f32[3,32,8,1]{3,2,1,0:T(8,128)S(1)}, f32[3,32,8,1]{3,2,1,0:T(8,128)S(1)}, u32[]{:S(2)}, u32[]{:S(2)}) collective-permute-start(f32[3,32,8,1]{3,2,1,0:T(8,128)S(1)} %slice.413), channel_id=1, source_target_pairs={{1,0},{2,1},{3,2},{5,4},{6,5},{7,6},{9,8},{10,9},{11,10},{13,12},{... | collective-permute-start | bytes 9224 | tf_op jit(solution)/shard_map/ppermute | solution.py:23
  3.0 11.0 %copy-start.20 = (f32[4]{0:T(128)S(1)}, f32[4]{0:T(128)}, u32[]{:S(2)}) copy-start(f32[4]{0:T(128)} %param.27) | copy-start | bytes 52
  3.0 12.8 %collective-permute-start = (f32[3,1,8,256]{3,2,1,0:T(8,128)S(1)}, f32[3,1,8,256]{3,2,1,0:T(8,128)S(1)}, u32[]{:S(2)}, u32[]{:S(2)}) collective-permute-start(f32[3,1,8,256]{3,2,1,0:T(8,128)S(1)} %slice.410), channel_id=1, source_target_pairs={{4,0},{8,4},{12,8},{16,12},{20,16},{24,20},{28,24},{32,28},{36,32}... | collective-permute-start | bytes 73736 | tf_op jit(solution)/shard_map/ppermute | solution.py:23
  17.2 9.6 %copy-start.13 = (s32[32,8,256]{2,1,0:T(8,128)S(1)}, s32[32,8,256]{2,1,0:T(8,128)}, u32[]{:S(2)}) copy-start(s32[32,8,256]{2,1,0:T(8,128)} %param.26) | copy-start | bytes 786436
  17.2 9.6 %copy-start.19 = (s32[32,8,256]{2,1,0:T(8,128)S(1)}, s32[32,8,256]{2,1,0:T(8,128)}, u32[]{:S(2)}) copy-start(s32[32,8,256]{2,1,0:T(8,128)} %param.25) | copy-start | bytes 786436
  17.4 13.0 %collective-permute-start.3 = (f32[3,32,8,1]{3,2,1,0:T(8,128)S(1)}, f32[3,32,8,1]{3,2,1,0:T(8,128)S(1)}, u32[]{:S(2)}, u32[]{:S(2)}) collective-permute-start(f32[3,32,8,1]{3,2,1,0:T(8,128)S(1)} %slice.423), channel_id=1, source_target_pairs={{0,1},{1,2},{2,3},{4,5},{5,6},{6,7},{8,9},{9,10},{10,11},{12,13},{... | collective-permute-start | bytes 9224 | tf_op jit(solution)/shard_map/ppermute | solution.py:23
  21.7 17.5 %collective-permute-start.2 = (f32[3,1,8,256]{3,2,1,0:T(8,128)S(1)}, f32[3,1,8,256]{3,2,1,0:T(8,128)S(1)}, u32[]{:S(2)}, u32[]{:S(2)}) collective-permute-start(f32[3,1,8,256]{3,2,1,0:T(8,128)S(1)} %slice.420), channel_id=1, source_target_pairs={{0,4},{4,8},{8,12},{12,16},{16,20},{20,24},{24,28},{28,32},{32,36}... | collective-permute-start | bytes 73736 | tf_op jit(solution)/shard_map/ppermute | solution.py:23
  39.6 1.1 copy-start.4
  42.4 3.4 %copy-start.5 = (f32[2,32,8,256]{3,2,1,0:T(8,128)S(1)}, f32[2,32,8,256]{3,2,1,0:T(8,128)}, u32[]{:S(2)}) copy-start(f32[2,32,8,256]{3,2,1,0:T(8,128)} %param.24) | copy-start | bytes 1572868
  42.5 9.8 %collective-permute-start.5 = (f32[3,32,8,1]{3,2,1,0:T(8,128)S(1)}, f32[3,32,8,1]{3,2,1,0:T(8,128)S(1)}, u32[]{:S(2)}, u32[]{:S(2)}) collective-permute-start(f32[3,32,8,1]{3,2,1,0:T(8,128)S(1)} %slice.437), channel_id=1, source_target_pairs={{1,0},{2,1},{3,2},{5,4},{6,5},{7,6},{9,8},{10,9},{11,10},{13,12},{... | collective-permute-start | bytes 9224 | tf_op jit(solution)/shard_map/ppermute | solution.py:23
  43.9 8.4 %collective-permute-start.4 = (f32[3,1,8,256]{3,2,1,0:T(8,128)S(1)}, f32[3,1,8,256]{3,2,1,0:T(8,128)S(1)}, u32[]{:S(2)}, u32[]{:S(2)}) collective-permute-start(f32[3,1,8,256]{3,2,1,0:T(8,128)S(1)} %slice.434), channel_id=1, source_target_pairs={{4,0},{8,4},{12,8},{16,12},{20,16},{24,20},{28,24},{32,28},{36,32}... | collective-permute-start | bytes 73736 | tf_op jit(solution)/shard_map/ppermute | solution.py:23
  53.0 9.7 %collective-permute-start.7 = (f32[3,32,8,1]{3,2,1,0:T(8,128)S(1)}, f32[3,32,8,1]{3,2,1,0:T(8,128)S(1)}, u32[]{:S(2)}, u32[]{:S(2)}) collective-permute-start(f32[3,32,8,1]{3,2,1,0:T(8,128)S(1)} %slice.447), channel_id=1, source_target_pairs={{0,1},{1,2},{2,3},{4,5},{5,6},{6,7},{8,9},{9,10},{10,11},{12,13},{... | collective-permute-start | bytes 9224 | tf_op jit(solution)/shard_map/ppermute | solution.py:23
  55.0 15.4 %collective-permute-start.6 = (f32[3,1,8,256]{3,2,1,0:T(8,128)S(1)}, f32[3,1,8,256]{3,2,1,0:T(8,128)S(1)}, u32[]{:S(2)}, u32[]{:S(2)}) collective-permute-start(f32[3,1,8,256]{3,2,1,0:T(8,128)S(1)} %slice.444), channel_id=1, source_target_pairs={{0,4},{4,8},{8,12},{12,16},{16,20},{20,24},{24,28},{28,32},{32,36}... | collective-permute-start | bytes 73736 | tf_op jit(solution)/shard_map/ppermute | solution.py:23
  71.6 1.1 copy-start.16
  73.2 1.1 copy-start.6
  73.2 1.4 copy-start.17
  73.3 1.3 copy-start.21
  75.1 9.7 %collective-permute-start.9 = (f32[3,32,8,1]{3,2,1,0:T(8,128)S(1)}, f32[3,32,8,1]{3,2,1,0:T(8,128)S(1)}, u32[]{:S(2)}, u32[]{:S(2)}) collective-permute-start(f32[3,32,8,1]{3,2,1,0:T(8,128)S(1)} %slice.461), channel_id=1, source_target_pairs={{1,0},{2,1},{3,2},{5,4},{6,5},{7,6},{9,8},{10,9},{11,10},{13,12},{... | collective-permute-start | bytes 9224 | tf_op jit(solution)/shard_map/ppermute | solution.py:23
  76.4 8.4 %collective-permute-start.8 = (f32[3,1,8,256]{3,2,1,0:T(8,128)S(1)}, f32[3,1,8,256]{3,2,1,0:T(8,128)S(1)}, u32[]{:S(2)}, u32[]{:S(2)}) collective-permute-start(f32[3,1,8,256]{3,2,1,0:T(8,128)S(1)} %slice.458), channel_id=1, source_target_pairs={{4,0},{8,4},{12,8},{16,12},{20,16},{24,20},{28,24},{32,28},{36,32}... | collective-permute-start | bytes 73736 | tf_op jit(solution)/shard_map/ppermute | solution.py:23
  85.1 1.3 copy-start.2
  85.3 17.9 %copy-start.7 = (f32[1,32,8,256]{3,2,1,0:T(8,128)}, f32[1,32,8,256]{3,2,1,0:T(8,128)S(1)}, u32[]{:S(2)}) copy-start(f32[1,32,8,256]{3,2,1,0:T(8,128)S(1)} %get-tuple-element.59) | copy-start | bytes 786436
  85.3 17.9 %copy-start.9 = (f32[1,32,8,256]{3,2,1,0:T(8,128)}, f32[1,32,8,256]{3,2,1,0:T(8,128)S(1)}, u32[]{:S(2)}) copy-start(f32[1,32,8,256]{3,2,1,0:T(8,128)S(1)} %get-tuple-element.60) | copy-start | bytes 786436
  85.3 17.9 %copy-start.11 = (f32[1,32,8,256]{3,2,1,0:T(8,128)}, f32[1,32,8,256]{3,2,1,0:T(8,128)S(1)}, u32[]{:S(2)}) copy-start(f32[1,32,8,256]{3,2,1,0:T(8,128)S(1)} %get-tuple-element.61) | copy-start | bytes 786436
  86.7 8.9 %collective-permute-start.11 = (f32[3,32,8,1]{3,2,1,0:T(8,128)S(1)}, f32[3,32,8,1]{3,2,1,0:T(8,128)S(1)}, u32[]{:S(2)}, u32[]{:S(2)}) collective-permute-start(f32[3,32,8,1]{3,2,1,0:T(8,128)S(1)} %slice.471), channel_id=1, source_target_pairs={{0,1},{1,2},{2,3},{4,5},{5,6},{6,7},{8,9},{9,10},{10,11},{12,13},{... | collective-permute-start | bytes 9224 | tf_op jit(solution)/shard_map/ppermute | solution.py:23
  88.8 14.5 %collective-permute-start.10 = (f32[3,1,8,256]{3,2,1,0:T(8,128)S(1)}, f32[3,1,8,256]{3,2,1,0:T(8,128)S(1)}, u32[]{:S(2)}, u32[]{:S(2)}) collective-permute-start(f32[3,1,8,256]{3,2,1,0:T(8,128)S(1)} %slice.468), channel_id=1, source_target_pairs={{0,4},{4,8},{8,12},{12,16},{16,20},{20,24},{24,28},{28,32},{32,36}... | collective-permute-start | bytes 73736 | tf_op jit(solution)/shard_map/ppermute | solution.py:23
  107.4 88.0 %collective-permute-start.13 = (f32[3,32,8,1]{3,2,1,0:T(8,128)}, f32[3,32,8,1]{3,2,1,0:T(8,128)}, u32[]{:S(2)}, u32[]{:S(2)}) collective-permute-start(f32[3,32,8,1]{3,2,1,0:T(8,128)} %slice.483), channel_id=1, source_target_pairs={{1,0},{2,1},{3,2},{5,4},{6,5},{7,6},{9,8},{10,9},{11,10},{13,12},{... | collective-permute-start | bytes 9224 | tf_op jit(solution)/shard_map/ppermute | solution.py:23
  108.7 86.7 %collective-permute-start.12 = (f32[3,1,8,256]{3,2,1,0:T(8,128)S(1)}, f32[3,1,8,256]{3,2,1,0:T(8,128)S(1)}, u32[]{:S(2)}, u32[]{:S(2)}) collective-permute-start(f32[3,1,8,256]{3,2,1,0:T(8,128)S(1)} %slice.480), channel_id=1, source_target_pairs={{4,0},{8,4},{12,8},{16,12},{20,16},{24,20},{28,24},{32,28},{36,32}... | collective-permute-start | bytes 73736 | tf_op jit(solution)/shard_map/ppermute | solution.py:23
  196.7 1.1 copy-start.12
  198.0 15.9 %copy-start.1 = (f32[3,32,8,256]{3,2,1,0:T(8,128)}, f32[3,32,8,256]{3,2,1,0:T(8,128)S(1)}, u32[]{:S(2)}) copy-start(f32[3,32,8,256]{3,2,1,0:T(8,128)S(1)} %maximum_add_fusion.1) | copy-start | bytes 2359300
  198.1 10.7 %collective-permute-start.15 = (f32[3,32,8,1]{3,2,1,0:T(8,128)S(1)}, f32[3,32,8,1]{3,2,1,0:T(8,128)S(1)}, u32[]{:S(2)}, u32[]{:S(2)}) collective-permute-start(f32[3,32,8,1]{3,2,1,0:T(8,128)S(1)} %slice.493), channel_id=1, source_target_pairs={{0,1},{1,2},{2,3},{4,5},{5,6},{6,7},{8,9},{9,10},{10,11},{12,13},{... | collective-permute-start | bytes 9224 | tf_op jit(solution)/shard_map/ppermute | solution.py:23
  200.2 13.7 %collective-permute-start.14 = (f32[3,1,8,256]{3,2,1,0:T(8,128)S(1)}, f32[3,1,8,256]{3,2,1,0:T(8,128)S(1)}, u32[]{:S(2)}, u32[]{:S(2)}) collective-permute-start(f32[3,1,8,256]{3,2,1,0:T(8,128)S(1)} %slice.490), channel_id=1, source_target_pairs={{0,4},{4,8},{8,12},{12,16},{16,20},{20,24},{24,28},{28,32},{32,36}... | collective-permute-start | bytes 73736 | tf_op jit(solution)/shard_map/ppermute | solution.py:23
  (7 other events, 6.5 us)
where the time goes:
time: 217 us; the launch traced here: 216 us
  blocking collectives  76.3 us (35%)
  waiting for transfers between devices  56.5 us (26%)
  starting transfers between devices  43.4 us (20%)
  other arithmetic  23.4 us (11%)
  local copies, waits for them, and re-layouts  13.7 us (6%)
  between operations  2.27 us (1%)
    psum x1, blocking collectives, step_total(): return lax.psum(label_sums(material_labels, values, count), ('gy', 'gz'))  76.3 us
    ppermute x16, waiting for transfers between devices, shifted(): return lax.ppermute(block, axis, route)  56.5 us
    ppermute x16, starting transfers between devices, shifted(): return lax.ppermute(block, axis, route)  43.4 us
    unnamed x46, local copies, waits for them, and re-layouts  8.78 us
    add x1, other arithmetic, on_device(): step_total(material_labels, grad_second, count)  5.11 us
  transfers between devices with their start and end apart: 16, of which 9 were waited for; matrix products, arithmetic and copies ran while one was open for 7% of the time, Pallas kernels for 0%

commit v1 on v0

--- a/solution.py
+++ b/solution.py
@@ -17,6 +17,11 @@
 SOURCE_OMEGA = 0.35
 
 
+def summed_here(shard, axis):
+    shards = lax.all_gather(shard, axis)
+    return jnp.sum(shards, axis=0)
+
+
 def shifted(block, axis, distance):
     devices = range(lax.axis_size(axis))
     route = [(i - distance, i) for i in devices if i - distance in devices]
@@ -109,7 +114,7 @@
 
 
 def step_total(material_labels, values, count):
-    return lax.psum(label_sums(material_labels, values, count), ("gy", "gz"))
+    return summed_here(label_sums(material_labels, values, count), ("gy", "gz"))
 
 
 def on_device(

time: 217 us -> 228 us (1.051)
  local copies, waits for them, and re-layouts: 13.7 us -> 22.2 us
  other arithmetic: 23.4 us -> 27.8 us
    unnamed x0 -> x1, blocking collectives: none -> 76.8 us
    psum x1 -> x0, blocking collectives: 76.3 us -> none  [step_total(): return lax.psum(label_sums(material_labels, values, count), ('gy', 'gz'))]
    unnamed x0 -> x2, other arithmetic: none -> 5.49 us
    add x1 -> x0, other arithmetic: 5.11 us -> none  [on_device(): step_total(material_labels, grad_second, count)]
    unnamed x46 -> x106, local copies, waits for them, and re-layouts: 8.78 us -> 12.4 us
  transfers between devices with their start and end apart: 16 -> 16, of which waited for: 9 -> 9; matrix products, arithmetic and copies ran while one was open for 7% -> 8% of each run, Pallas kernels for 0% -> 0%
where the time goes in v1:
time: 228 us; the launch traced here: 227 us
  blocking collectives  76.8 us (34%)
  waiting for transfers between devices  55.3 us (24%)
  starting transfers between devices  42.7 us (19%)
  other arithmetic  27.8 us (12%)
  local copies, waits for them, and re-layouts  22.2 us (10%)
  between operations  2.53 us (1%)
    unnamed x1, blocking collectives  76.8 us
    ppermute x16, waiting for transfers between devices, shifted(): return lax.ppermute(block, axis, route)  55.3 us
    ppermute x16, starting transfers between devices, shifted(): return lax.ppermute(block, axis, route)  42.7 us
    unnamed x106, local copies, waits for them, and re-layouts  12.4 us
    unnamed x2, other arithmetic  5.49 us
  transfers between devices with their start and end apart: 16, of which 9 were waited for; matrix products, arithmetic and copies ran while one was open for 8% of the time, Pallas kernels for 0%

profile of v1, /device:TPU:2, one launch (start us, length us, event | category | flops | bytes accessed | tf_op | source)
XLA Modules:
  0.0 227.3 jit_solution(12572453001096764230)
XLA Ops:
  1.7 1.3 collective-permute-start.1
  3.0 11.0 %collective-permute-start = (f32[3,1,8,256]{3,2,1,0:T(8,128)S(1)}, f32[3,1,8,256]{3,2,1,0:T(8,128)S(1)}, u32[]{:S(2)}, u32[]{:S(2)}) collective-permute-start(f32[3,1,8,256]{3,2,1,0:T(8,128)S(1)} %slice.410), channel_id=1, source_target_pairs={{4,0},{8,4},{12,8},{16,12},{20,16},{24,20},{28,24},{32,28},{36,32}... | collective-permute-start | bytes 73736 | tf_op jit(solution)/shard_map/ppermute | solution.py:28
  17.5 4.3 %collective-permute-start.3 = (f32[3,32,8,1]{3,2,1,0:T(8,128)S(1)}, f32[3,32,8,1]{3,2,1,0:T(8,128)S(1)}, u32[]{:S(2)}, u32[]{:S(2)}) collective-permute-start(f32[3,32,8,1]{3,2,1,0:T(8,128)S(1)} %slice.423), channel_id=1, source_target_pairs={{0,1},{1,2},{2,3},{4,5},{5,6},{6,7},{8,9},{9,10},{10,11},{12,13},{... | collective-permute-start | bytes 9224 | tf_op jit(solution)/shard_map/ppermute | solution.py:28
  21.8 5.1 %collective-permute-start.2 = (f32[3,1,8,256]{3,2,1,0:T(8,128)S(1)}, f32[3,1,8,256]{3,2,1,0:T(8,128)S(1)}, u32[]{:S(2)}, u32[]{:S(2)}) collective-permute-start(f32[3,1,8,256]{3,2,1,0:T(8,128)S(1)} %slice.420), channel_id=1, source_target_pairs={{0,4},{4,8},{8,12},{12,16},{16,20},{20,24},{24,28},{28,32},{32,36}... | collective-permute-start | bytes 73736 | tf_op jit(solution)/shard_map/ppermute | solution.py:28
  26.9 3.5 %select_add_fusion.2 = (f32[32,8,256]{2,1,0:T(8,128)S(1)}, pred[32,8,256]{2,1,0:T(8,128)(4,1)}, pred[32,8,256]{2,1,0:T(8,128)(4,1)}, pred[32,8,256]{2,1,0:T(8,12...) fusion(f32[]{:T(128)} %bitcast.6, f32[]{:T(128)} %bitcast.5, f32[]{:T(128)} %bitcast.4, f32[]{:T(128)} %bitcast.3, ...), kind=kLoop, calls=%fused_computation.118 | loop fusion | flops 983040 | bytes 1835024 | tf_op jit(solution)/shard_map/add | solution.py:101
  31.2 8.1 %collective-permute-done.2 = f32[3,1,8,256]{3,2,1,0:T(8,128)S(1)} collective-permute-done((f32[3,1,8,256]{3,2,1,0:T(8,128)S(1)}, f32[3,1,8,256]{3,2,1,0:T(8,128)S(1)}, u32[]{:S(2)}, u32[]{:S(2)}) %collective-permute-start.2) | collective-permute-done | bytes 24608 | tf_op jit(solution)/shard_map/ppermute | solution.py:28
  45.9 1.9 collective-permute-start.4
  49.2 5.3 %collective-permute-done.5 = f32[3,32,8,1]{3,2,1,0:T(8,128)} collective-permute-done((f32[3,32,8,1]{3,2,1,0:T(8,128)}, f32[3,32,8,1]{3,2,1,0:T(8,128)}, u32[]{:S(2)}, u32[]{:S(2)}) %collective-permute-start.5) | collective-permute-done | bytes 3104 | tf_op jit(solution)/shard_map/ppermute | solution.py:28
  54.6 1.3 maximum_subtract_fusion.3
  57.4 2.0 collective-permute-start.7
  59.5 1.9 collective-permute-start.6
  61.7 5.6 %collective-permute-done.7 = f32[3,32,8,1]{3,2,1,0:T(8,128)S(1)} collective-permute-done((f32[3,32,8,1]{3,2,1,0:T(8,128)S(1)}, f32[3,32,8,1]{3,2,1,0:T(8,128)S(1)}, u32[]{:S(2)}, u32[]{:S(2)}) %collective-permute-start.7) | collective-permute-done | bytes 3104 | tf_op jit(solution)/shard_map/ppermute | solution.py:28
  67.3 7.4 %collective-permute-done.6 = f32[3,1,8,256]{3,2,1,0:T(8,128)S(1)} collective-permute-done((f32[3,1,8,256]{3,2,1,0:T(8,128)S(1)}, f32[3,1,8,256]{3,2,1,0:T(8,128)S(1)}, u32[]{:S(2)}, u32[]{:S(2)}) %collective-permute-start.6) | collective-permute-done | bytes 24608 | tf_op jit(solution)/shard_map/ppermute | solution.py:28
  79.6 1.3 collective-permute-start.9
  80.9 1.9 collective-permute-start.8
  84.6 4.7 %collective-permute-done.9 = f32[3,32,8,1]{3,2,1,0:T(8,128)S(1)} collective-permute-done((f32[3,32,8,1]{3,2,1,0:T(8,128)S(1)}, f32[3,32,8,1]{3,2,1,0:T(8,128)S(1)}, u32[]{:S(2)}, u32[]{:S(2)}) %collective-permute-start.9) | collective-permute-done | bytes 3104 | tf_op jit(solution)/shard_map/ppermute | solution.py:28
  91.2 1.8 collective-permute-start.11
  93.0 1.9 collective-permute-start.10
  95.1 5.3 %collective-permute-done.11 = f32[3,32,8,1]{3,2,1,0:T(8,128)S(1)} collective-permute-done((f32[3,32,8,1]{3,2,1,0:T(8,128)S(1)}, f32[3,32,8,1]{3,2,1,0:T(8,128)S(1)}, u32[]{:S(2)}, u32[]{:S(2)}) %collective-permute-start.11) | collective-permute-done | bytes 3104 | tf_op jit(solution)/shard_map/ppermute | solution.py:28
  100.4 7.1 %collective-permute-done.10 = f32[3,1,8,256]{3,2,1,0:T(8,128)S(1)} collective-permute-done((f32[3,1,8,256]{3,2,1,0:T(8,128)S(1)}, f32[3,1,8,256]{3,2,1,0:T(8,128)S(1)}, u32[]{:S(2)}, u32[]{:S(2)}) %collective-permute-start.10) | collective-permute-done | bytes 24608 | tf_op jit(solution)/shard_map/ppermute | solution.py:28
  110.5 1.6 multiply_add_fusion
  113.5 1.4 collective-permute-start.13
  115.0 1.9 collective-permute-start.12
  117.0 1.6 select_reduce_fusion.7
  118.5 2.8 %maximum_dynamic-update-slice_fusion.1 = f32[1024]{0:T(1024)S(1)} fusion(f32[1024]{0:T(1024)S(1)} %broadcast.161.clone.1, u32[]{:T(128)S(6)} %multiply.9, f32[1]{0:T(128)} %bitcast.23, f32[1]{0:T(128)} %bitcast.22, f32[1]{0:T(128)} %bitcast.21, f32[1]{0:T(128)} %bitcast.20), kind=kLoop, calls=%fused_computation.133 | loop fusion | flops 12 | bytes 532
  122.5 2.7 %maximum_dynamic-update-slice_fusion = f32[1024]{0:T(1024)S(1)} fusion(f32[1024]{0:T(1024)S(1)} %broadcast.161.clone, u32[]{:T(128)S(6)} %multiply.9, f32[1]{0:T(128)} %bitcast.19, f32[1]{0:T(128)} %bitcast.18, f32[1]{0:T(128)} %bitcast.17, f32[1]{0:T(128)} %bitcast.16), kind=kLoop, calls=%fused_computation.132 | loop fusion | flops 12 | bytes 532
  128.3 76.8 %all-reduce.28 = (f32[1024]{0:T(1024)S(1)}, f32[1024]{0:T(1024)S(1)}) all-reduce(f32[1024]{0:T(1024)S(1)} %maximum_dynamic-update-slice_fusion, f32[1024]{0:T(1024)S(1)} %maximum_dynamic-update-slice_fusion.1), channel_id=2, replica_groups=mesh['gy'=64,'gz'=4] {'gy','gz'}, use_global_device_ids=true, to_apply=%add.26 | all-reduce | flops 2048 | bytes 16384
  205.4 2.0 maximum_subtract_fusion.11
  208.8 1.6 collective-permute-start.15
  210.4 1.9 collective-permute-start.14
  212.9 6.1 %collective-permute-done.15 = f32[3,32,8,1]{3,2,1,0:T(8,128)S(1)} collective-permute-done((f32[3,32,8,1]{3,2,1,0:T(8,128)S(1)}, f32[3,32,8,1]{3,2,1,0:T(8,128)S(1)}, u32[]{:S(2)}, u32[]{:S(2)}) %collective-permute-start.15) | collective-permute-done | bytes 3104 | tf_op jit(solution)/shard_map/ppermute | solution.py:28
  219.0 5.6 %collective-permute-done.14 = f32[3,1,8,256]{3,2,1,0:T(8,128)S(1)} collective-permute-done((f32[3,1,8,256]{3,2,1,0:T(8,128)S(1)}, f32[3,1,8,256]{3,2,1,0:T(8,128)S(1)}, u32[]{:S(2)}, u32[]{:S(2)}) %collective-permute-start.14) | collective-permute-done | bytes 24608 | tf_op jit(solution)/shard_map/ppermute | solution.py:28
  (195 shorter events, 35.9 us)
Async XLA Ops:
  1.7 14.2 %collective-permute-start.1 = (f32[3,32,8,1]{3,2,1,0:T(8,128)S(1)}, f32[3,32,8,1]{3,2,1,0:T(8,128)S(1)}, u32[]{:S(2)}, u32[]{:S(2)}) collective-permute-start(f32[3,32,8,1]{3,2,1,0:T(8,128)S(1)} %slice.413), channel_id=1, source_target_pairs={{1,0},{2,1},{3,2},{5,4},{6,5},{7,6},{9,8},{10,9},{11,10},{13,12},{... | collective-permute-start | bytes 9224 | tf_op jit(solution)/shard_map/ppermute | solution.py:28
  3.0 11.0 %copy-start.49 = (f32[4]{0:T(128)S(1)}, f32[4]{0:T(128)}, u32[]{:S(2)}) copy-start(f32[4]{0:T(128)} %param.27) | copy-start | bytes 52
  3.0 12.9 %collective-permute-start = (f32[3,1,8,256]{3,2,1,0:T(8,128)S(1)}, f32[3,1,8,256]{3,2,1,0:T(8,128)S(1)}, u32[]{:S(2)}, u32[]{:S(2)}) collective-permute-start(f32[3,1,8,256]{3,2,1,0:T(8,128)S(1)} %slice.410), channel_id=1, source_target_pairs={{4,0},{8,4},{12,8},{16,12},{20,16},{24,20},{28,24},{32,28},{36,32}... | collective-permute-start | bytes 73736 | tf_op jit(solution)/shard_map/ppermute | solution.py:28
  15.8 11.0 %copy-start.26 = (f32[2,32,8,256]{3,2,1,0:T(8,128)}, f32[2,32,8,256]{3,2,1,0:T(8,128)S(1)}, u32[]{:S(2)}) copy-start(f32[2,32,8,256]{3,2,1,0:T(8,128)S(1)} %convert_element_type.25) | copy-start | bytes 1572868
  16.3 23.0 %copy-start.12 = (f32[1,32,8,256]{3,2,1,0:T(8,128)}, f32[1,32,8,256]{3,2,1,0:T(8,128)S(1)}, u32[]{:S(2)}) copy-start(f32[1,32,8,256]{3,2,1,0:T(8,128)S(1)} %get-tuple-element.83) | copy-start | bytes 786436
  16.3 23.0 %copy-start.14 = (f32[1,32,8,256]{3,2,1,0:T(8,128)}, f32[1,32,8,256]{3,2,1,0:T(8,128)S(1)}, u32[]{:S(2)}) copy-start(f32[1,32,8,256]{3,2,1,0:T(8,128)S(1)} %get-tuple-element.84) | copy-start | bytes 786436
  17.3 9.6 %copy-start.20 = (s32[32,8,256]{2,1,0:T(8,128)S(1)}, s32[32,8,256]{2,1,0:T(8,128)}, u32[]{:S(2)}) copy-start(s32[32,8,256]{2,1,0:T(8,128)} %param.26) | copy-start | bytes 786436
  17.3 9.6 %copy-start.48 = (s32[32,8,256]{2,1,0:T(8,128)S(1)}, s32[32,8,256]{2,1,0:T(8,128)}, u32[]{:S(2)}) copy-start(s32[32,8,256]{2,1,0:T(8,128)} %param.25) | copy-start | bytes 786436
  17.5 13.7 %collective-permute-start.3 = (f32[3,32,8,1]{3,2,1,0:T(8,128)S(1)}, f32[3,32,8,1]{3,2,1,0:T(8,128)S(1)}, u32[]{:S(2)}, u32[]{:S(2)}) collective-permute-start(f32[3,32,8,1]{3,2,1,0:T(8,128)S(1)} %slice.423), channel_id=1, source_target_pairs={{0,1},{1,2},{2,3},{4,5},{5,6},{6,7},{8,9},{9,10},{10,11},{12,13},{... | collective-permute-start | bytes 9224 | tf_op jit(solution)/shard_map/ppermute | solution.py:28
  21.8 17.5 %collective-permute-start.2 = (f32[3,1,8,256]{3,2,1,0:T(8,128)S(1)}, f32[3,1,8,256]{3,2,1,0:T(8,128)S(1)}, u32[]{:S(2)}, u32[]{:S(2)}) collective-permute-start(f32[3,1,8,256]{3,2,1,0:T(8,128)S(1)} %slice.420), channel_id=1, source_target_pairs={{0,4},{4,8},{8,12},{12,16},{16,20},{20,24},{24,28},{28,32},{32,36}... | collective-permute-start | bytes 73736 | tf_op jit(solution)/shard_map/ppermute | solution.py:28
  43.2 4.6 %copy-start.7 = (f32[2,32,8,256]{3,2,1,0:T(8,128)S(1)}, f32[2,32,8,256]{3,2,1,0:T(8,128)}, u32[]{:S(2)}) copy-start(f32[2,32,8,256]{3,2,1,0:T(8,128)} %param.24) | copy-start | bytes 1572868
  44.6 10.0 %collective-permute-start.5 = (f32[3,32,8,1]{3,2,1,0:T(8,128)}, f32[3,32,8,1]{3,2,1,0:T(8,128)}, u32[]{:S(2)}, u32[]{:S(2)}) collective-permute-start(f32[3,32,8,1]{3,2,1,0:T(8,128)} %slice.437), channel_id=1, source_target_pairs={{1,0},{2,1},{3,2},{5,4},{6,5},{7,6},{9,8},{10,9},{11,10},{13,12},{... | collective-permute-start | bytes 9224 | tf_op jit(solution)/shard_map/ppermute | solution.py:28
  45.9 8.7 %collective-permute-start.4 = (f32[3,1,8,256]{3,2,1,0:T(8,128)}, f32[3,1,8,256]{3,2,1,0:T(8,128)}, u32[]{:S(2)}, u32[]{:S(2)}) collective-permute-start(f32[3,1,8,256]{3,2,1,0:T(8,128)} %slice.434), channel_id=1, source_target_pairs={{4,0},{8,4},{12,8},{16,12},{20,16},{24,20},{28,24},{32,28},{36,32}... | collective-permute-start | bytes 73736 | tf_op jit(solution)/shard_map/ppermute | solution.py:28
  48.7 34.1 %copy-start.28 = (f32[1,32,8,256]{3,2,1,0:T(8,128)}, f32[1,32,8,256]{3,2,1,0:T(8,128)S(1)}, u32[]{:S(2)}) copy-start(f32[1,32,8,256]{3,2,1,0:T(8,128)S(1)} %get-tuple-element.93) | copy-start | bytes 786436
  48.7 34.2 %copy-start.30 = (f32[1,32,8,256]{3,2,1,0:T(8,128)}, f32[1,32,8,256]{3,2,1,0:T(8,128)S(1)}, u32[]{:S(2)}) copy-start(f32[1,32,8,256]{3,2,1,0:T(8,128)S(1)} %get-tuple-element.94) | copy-start | bytes 786436
  48.7 34.2 %copy-start.32 = (f32[1,32,8,256]{3,2,1,0:T(8,128)}, f32[1,32,8,256]{3,2,1,0:T(8,128)S(1)}, u32[]{:S(2)}) copy-start(f32[1,32,8,256]{3,2,1,0:T(8,128)S(1)} %get-tuple-element.95) | copy-start | bytes 786436
  57.0 4.4 %copy-start.40 = (f32[32,8,256]{2,1,0:T(8,128)S(1)}, f32[32,8,256]{2,1,0:T(8,128)}, u32[]{:S(2)}) copy-start(f32[32,8,256]{2,1,0:T(8,128)} %get-tuple-element.29) | copy-start | bytes 786436
  57.4 9.9 %collective-permute-start.7 = (f32[3,32,8,1]{3,2,1,0:T(8,128)S(1)}, f32[3,32,8,1]{3,2,1,0:T(8,128)S(1)}, u32[]{:S(2)}, u32[]{:S(2)}) collective-permute-start(f32[3,32,8,1]{3,2,1,0:T(8,128)S(1)} %slice.447), channel_id=1, source_target_pairs={{0,1},{1,2},{2,3},{4,5},{5,6},{6,7},{8,9},{9,10},{10,11},{12,13},{... | collective-permute-start | bytes 9224 | tf_op jit(solution)/shard_map/ppermute | solution.py:28
  59.5 15.3 %collective-permute-start.6 = (f32[3,1,8,256]{3,2,1,0:T(8,128)S(1)}, f32[3,1,8,256]{3,2,1,0:T(8,128)S(1)}, u32[]{:S(2)}, u32[]{:S(2)}) collective-permute-start(f32[3,1,8,256]{3,2,1,0:T(8,128)S(1)} %slice.444), channel_id=1, source_target_pairs={{0,4},{4,8},{8,12},{12,16},{16,20},{20,24},{24,28},{28,32},{32,36}... | collective-permute-start | bytes 73736 | tf_op jit(solution)/shard_map/ppermute | solution.py:28
  79.6 9.7 %collective-permute-start.9 = (f32[3,32,8,1]{3,2,1,0:T(8,128)S(1)}, f32[3,32,8,1]{3,2,1,0:T(8,128)S(1)}, u32[]{:S(2)}, u32[]{:S(2)}) collective-permute-start(f32[3,32,8,1]{3,2,1,0:T(8,128)S(1)} %slice.461), channel_id=1, source_target_pairs={{1,0},{2,1},{3,2},{5,4},{6,5},{7,6},{9,8},{10,9},{11,10},{13,12},{... | collective-permute-start | bytes 9224 | tf_op jit(solution)/shard_map/ppermute | solution.py:28
  80.9 8.4 %collective-permute-start.8 = (f32[3,1,8,256]{3,2,1,0:T(8,128)S(1)}, f32[3,1,8,256]{3,2,1,0:T(8,128)S(1)}, u32[]{:S(2)}, u32[]{:S(2)}) collective-permute-start(f32[3,1,8,256]{3,2,1,0:T(8,128)S(1)} %slice.458), channel_id=1, source_target_pairs={{4,0},{8,4},{12,8},{16,12},{20,16},{24,20},{28,24},{32,28},{36,32}... | collective-permute-start | bytes 73736 | tf_op jit(solution)/shard_map/ppermute | solution.py:28
  89.7 17.8 %copy-start.16 = (f32[1,32,8,256]{3,2,1,0:T(8,128)}, f32[1,32,8,256]{3,2,1,0:T(8,128)S(1)}, u32[]{:S(2)}) copy-start(f32[1,32,8,256]{3,2,1,0:T(8,128)S(1)} %get-tuple-element.62) | copy-start | bytes 786436
  89.7 17.8 %copy-start.18 = (f32[1,32,8,256]{3,2,1,0:T(8,128)}, f32[1,32,8,256]{3,2,1,0:T(8,128)S(1)}, u32[]{:S(2)}) copy-start(f32[1,32,8,256]{3,2,1,0:T(8,128)S(1)} %get-tuple-element.63) | copy-start | bytes 786436
  91.2 9.2 %collective-permute-start.11 = (f32[3,32,8,1]{3,2,1,0:T(8,128)S(1)}, f32[3,32,8,1]{3,2,1,0:T(8,128)S(1)}, u32[]{:S(2)}, u32[]{:S(2)}) collective-permute-start(f32[3,32,8,1]{3,2,1,0:T(8,128)S(1)} %slice.471), channel_id=1, source_target_pairs={{0,1},{1,2},{2,3},{4,5},{5,6},{6,7},{8,9},{9,10},{10,11},{12,13},{... | collective-permute-start | bytes 9224 | tf_op jit(solution)/shard_map/ppermute | solution.py:28
  93.0 14.4 %collective-permute-start.10 = (f32[3,1,8,256]{3,2,1,0:T(8,128)S(1)}, f32[3,1,8,256]{3,2,1,0:T(8,128)S(1)}, u32[]{:S(2)}, u32[]{:S(2)}) collective-permute-start(f32[3,1,8,256]{3,2,1,0:T(8,128)S(1)} %slice.468), channel_id=1, source_target_pairs={{0,4},{4,8},{8,12},{12,16},{16,20},{20,24},{24,28},{28,32},{32,36}... | collective-permute-start | bytes 73736 | tf_op jit(solution)/shard_map/ppermute | solution.py:28
  113.5 91.9 %collective-permute-start.13 = (f32[3,32,8,1]{3,2,1,0:T(8,128)}, f32[3,32,8,1]{3,2,1,0:T(8,128)}, u32[]{:S(2)}, u32[]{:S(2)}) collective-permute-start(f32[3,32,8,1]{3,2,1,0:T(8,128)} %slice.483), channel_id=1, source_target_pairs={{1,0},{2,1},{3,2},{5,4},{6,5},{7,6},{9,8},{10,9},{11,10},{13,12},{... | collective-permute-start | bytes 9224 | tf_op jit(solution)/shard_map/ppermute | solution.py:28
  115.0 90.5 %collective-permute-start.12 = (f32[3,1,8,256]{3,2,1,0:T(8,128)}, f32[3,1,8,256]{3,2,1,0:T(8,128)}, u32[]{:S(2)}, u32[]{:S(2)}) collective-permute-start(f32[3,1,8,256]{3,2,1,0:T(8,128)} %slice.480), channel_id=1, source_target_pairs={{4,0},{8,4},{12,8},{16,12},{20,16},{24,20},{28,24},{32,28},{36,32}... | collective-permute-start | bytes 73736 | tf_op jit(solution)/shard_map/ppermute | solution.py:28
  116.9 4.4 %copy-start.29 = (f32[1,32,8,256]{3,2,1,0:T(8,128)S(1)}, f32[1,32,8,256]{3,2,1,0:T(8,128)}, u32[]{:S(2)}) copy-start(f32[1,32,8,256]{3,2,1,0:T(8,128)} %copy-done.28) | copy-start | bytes 786436
  116.9 4.4 %copy-start.31 = (f32[1,32,8,256]{3,2,1,0:T(8,128)S(1)}, f32[1,32,8,256]{3,2,1,0:T(8,128)}, u32[]{:S(2)}) copy-start(f32[1,32,8,256]{3,2,1,0:T(8,128)} %copy-done.30) | copy-start | bytes 786436
  208.6 16.0 %copy-start.1 = (f32[3,32,8,256]{3,2,1,0:T(8,128)}, f32[3,32,8,256]{3,2,1,0:T(8,128)S(1)}, u32[]{:S(2)}) copy-start(f32[3,32,8,256]{3,2,1,0:T(8,128)S(1)} %maximum_add_fusion.1) | copy-start | bytes 2359300
  208.8 10.2 %collective-permute-start.15 = (f32[3,32,8,1]{3,2,1,0:T(8,128)S(1)}, f32[3,32,8,1]{3,2,1,0:T(8,128)S(1)}, u32[]{:S(2)}, u32[]{:S(2)}) collective-permute-start(f32[3,32,8,1]{3,2,1,0:T(8,128)S(1)} %slice.493), channel_id=1, source_target_pairs={{0,1},{1,2},{2,3},{4,5},{5,6},{6,7},{8,9},{9,10},{10,11},{12,13},{... | collective-permute-start | bytes 9224 | tf_op jit(solution)/shard_map/ppermute | solution.py:28
  210.4 14.2 %collective-permute-start.14 = (f32[3,1,8,256]{3,2,1,0:T(8,128)S(1)}, f32[3,1,8,256]{3,2,1,0:T(8,128)S(1)}, u32[]{:S(2)}, u32[]{:S(2)}) collective-permute-start(f32[3,1,8,256]{3,2,1,0:T(8,128)S(1)} %slice.490), channel_id=1, source_target_pairs={{0,4},{4,8},{8,12},{12,16},{16,20},{20,24},{24,28},{28,32},{32,36}... | collective-permute-start | bytes 73736 | tf_op jit(solution)/shard_map/ppermute | solution.py:28
  (36 other events, 63.1 us)
